TPU v7x, 128 devices: a whole 4x4x4 slice. The times are simulated.
128 devices in a mesh: row: 16 (over y, z_lo, core), col: 8 (over z_hi, x).
Axes of the slice: x: 4, y: 4, z: 4 (z_hi: 2, z_lo: 2; z = z_hi * 2 + z_lo), core: 2. Of those that a mesh axis runs over, the one named last changes fastest.
Arguments:
- z_trunk: bfloat16 [1024, 1024, 128], P('row', 'col'), may hold values from -6 to 6
- coords: int32 [3, 1024], P(None, ('row', 'col')), may hold values from 0 to 255
- token_mask: int32 [1024], P(('row', 'col')), may hold values 0 or 1
- w_dist: bfloat16 [39, 128], replicated, may hold values from -6 to 6
- w_attn: bfloat16 [128, 512], replicated, may hold values from -0.5 to 0.5
- w_bias: bfloat16 [128, 4], replicated, may hold values from -100 to 100
- w_out: bfloat16 [128, 128], replicated, may hold values from -2 to 2
- w_pae: bfloat16 [128, 64], replicated, may hold values from -0.5 to 0.5
- w_pde: bfloat16 [128, 64], replicated, may hold values from -0.5 to 0.5
Outputs:
- logits: float32 [1024, 1024, 128], P('row', 'col')
All inputs are finite; a program needn't handle non-finite values. No bound on the sum of `token_mask` on one device may be relied on, other than what follows from the above.
Results may differ from a plain program's by a relative error of at most 0.0055.
The roundings to bfloat16 on the way count: a program that leaves them out, or rounds other values in their place, can miss the bound.
Values may be sent and summed in bfloat16 or wider, within the bound.
A program may use at most 192 MiB of HBM per device.

v0:
```python
import jax
import jax.numpy as jnp
from jax import lax
from jax.sharding import PartitionSpec as P


def layer_norm(values):
    widened = values.astype(jnp.float32)
    average = jnp.mean(widened, axis=-1, keepdims=True)
    centred = widened - average
    variance = jnp.mean(centred * centred, axis=-1, keepdims=True)
    return (centred * lax.rsqrt(variance + 1e-05)).astype(jnp.bfloat16)


def distance_bins(coord_rows, coord_cols, class_count):
    offsets = coord_rows[:, :, None] - coord_cols[:, None, :]
    squared = jnp.sum(offsets * offsets, axis=0)
    bin_edges = 27 + 4 * jnp.arange(class_count - 1, dtype=jnp.int32)
    above = (squared[:, :, None] > (bin_edges * bin_edges)[None, None, :]).astype(jnp.int32)
    return jnp.sum(above, axis=-1)


def attend_column(query_rows, key_rows, value_rows, bias_full, key_bias):
    length_all = query_rows.shape[0]
    block_rows = min(512, length_all)

    def one_block(first_row):
        query_block = lax.dynamic_slice_in_dim(query_rows, first_row, block_rows, 0)
        bias_block = lax.dynamic_slice_in_dim(bias_full, first_row, block_rows, 2)
        scores = jnp.einsum(
            "khd,ihd->hki", key_rows, query_block, preferred_element_type=jnp.float32
        )
        scores = scores + bias_block + key_bias[None, :, None]
        highest = jnp.max(scores, axis=1, keepdims=True)
        raised = jnp.exp(scores - highest)
        weights = (raised / jnp.sum(raised, axis=1, keepdims=True)).astype(jnp.bfloat16)
        return jnp.einsum("hki,khd->ihd", weights, value_rows, preferred_element_type=jnp.float32)

    starts = jnp.arange(length_all // block_rows, dtype=jnp.int32) * block_rows
    blocks_out = lax.map(one_block, starts)
    return blocks_out.reshape(length_all, query_rows.shape[1], query_rows.shape[2])


def error_logits(updated, mirrored, w_pae, w_pde):
    width = updated.shape[-1]
    symmetric = updated.astype(jnp.float32) + mirrored.astype(jnp.float32)
    pae_part = jnp.dot(
        layer_norm(updated).reshape(-1, width), w_pae, preferred_element_type=jnp.float32
    )
    pde_part = jnp.dot(
        layer_norm(symmetric).reshape(-1, width), w_pde, preferred_element_type=jnp.float32
    )
    return jnp.concatenate([pae_part, pde_part], axis=1).reshape(
        updated.shape[0], updated.shape[1], -1
    )


def per_device(z_trunk, coords, token_mask, w_dist, w_attn, w_bias, w_out, w_pae, w_pde):
    all_coords, all_mask = (
        lax.all_gather(coords, ("row", "col"), axis=1, tiled=True),
        lax.all_gather(token_mask, ("row", "col"), axis=0, tiled=True),
    )
    rows_dev = z_trunk.shape[0]
    cols_dev = z_trunk.shape[1]
    width = z_trunk.shape[2]
    n_rows = lax.axis_size("row")
    n_cols = lax.axis_size("col")
    total = rows_dev * n_rows
    slab = rows_dev // n_cols
    heads = w_bias.shape[1]
    head_dim = width // heads
    classes = w_dist.shape[0]
    row_first = lax.axis_index("row") * rows_dev
    col_first = lax.axis_index("col") * cols_dev
    coord_rows = lax.dynamic_slice_in_dim(all_coords, row_first, rows_dev, 1)
    coord_cols = lax.dynamic_slice_in_dim(all_coords, col_first, cols_dev, 1)
    bins_tile = distance_bins(coord_rows, coord_cols, classes)
    one_hot = (bins_tile[:, :, None] == jnp.arange(classes, dtype=jnp.int32)[None, None, :]).astype(
        jnp.bfloat16
    )
    embedded = jnp.dot(one_hot.reshape(-1, classes), w_dist, preferred_element_type=jnp.float32)
    pair = (z_trunk.astype(jnp.float32) + embedded.reshape(rows_dev, cols_dev, width)).astype(
        jnp.bfloat16
    )
    pair_cols = lax.all_to_all(pair, "row", split_axis=1, concat_axis=0, tiled=True)
    normed = layer_norm(pair_cols)
    flat_normed = normed.reshape(-1, width)
    projected = jnp.dot(flat_normed, w_attn, preferred_element_type=jnp.float32)
    query_all = (
        (projected[:, :width] * head_dim ** (-0.5))
        .astype(jnp.bfloat16)
        .reshape(total, slab, heads, head_dim)
    )
    key_all = (
        projected[:, width : 2 * width].astype(jnp.bfloat16).reshape(total, slab, heads, head_dim)
    )
    value_all = (
        projected[:, 2 * width : 3 * width]
        .astype(jnp.bfloat16)
        .reshape(total, slab, heads, head_dim)
    )
    gate_all = projected[:, 3 * width :].astype(jnp.bfloat16)
    bias_local = jnp.einsum("kic,ch->hki", normed, w_bias, preferred_element_type=jnp.float32)
    gathered = lax.all_gather(bias_local, ("row", "col"), axis=2, tiled=True)
    bias_full = (
        gathered.reshape(heads, total, n_rows, n_cols, slab)
        .transpose(0, 1, 3, 2, 4)
        .reshape(heads, total, total)
    )
    key_bias = (all_mask.astype(jnp.float32) - 1.0) * 30000.0

    def one_column(operands):
        query_rows, key_rows, value_rows = operands
        return attend_column(query_rows, key_rows, value_rows, bias_full, key_bias)

    attended = lax.map(
        one_column,
        (jnp.swapaxes(query_all, 0, 1), jnp.swapaxes(key_all, 0, 1), jnp.swapaxes(value_all, 0, 1)),
    )
    attended = jnp.swapaxes(attended, 0, 1).reshape(total * slab, width)
    gated = (jax.nn.sigmoid(gate_all.astype(jnp.float32)) * attended).astype(jnp.bfloat16)
    update = jnp.dot(gated, w_out, preferred_element_type=jnp.float32)
    updated = (pair_cols.reshape(-1, width).astype(jnp.float32) + update).astype(jnp.bfloat16)
    updated = updated.reshape(total, slab, width)
    pieces = updated.reshape(n_cols, n_rows, slab, slab, width).transpose(1, 0, 2, 3, 4)
    flat_pieces = pieces.reshape(n_rows * n_cols, slab, slab, width)
    moved = lax.all_to_all(flat_pieces, ("row", "col"), split_axis=0, concat_axis=0, tiled=True)
    moved = moved.reshape(n_rows, n_cols, slab, slab, width)
    mirrored = moved.transpose(1, 0, 3, 2, 4).reshape(total, slab, width)
    logits_cols = error_logits(updated, mirrored, w_pae, w_pde)
    return lax.all_to_all(
        logits_cols.astype(jnp.bfloat16), "row", split_axis=0, concat_axis=1, tiled=True
    ).astype(logits_cols.dtype)


def solution(mesh):
    in_specs = (
        P("row", "col", None),
        P(None, ("row", "col")),
        P(("row", "col")),
        P(),
        P(),
        P(),
        P(),
        P(),
        P(),
    )
    out_specs = P("row", "col", None)
    return jax.shard_map(
        per_device, mesh=mesh, in_specs=in_specs, out_specs=out_specs, check_vma=False
    )
```

profile of v0, /device:TPU:1, one launch (start us, length us, event | category | flops | bytes accessed | tf_op | source)
XLA Modules:
  0.0 1159.6 jit_solution(17012444799415025751)
XLA Ops:
  6.5 305.9 %all-gather = s32[128,8,3]{1,2,0:T(4,128)S(1)} all-gather(s32[1,8,3]{1,2,0:T(4,128)} %bitcast.145), channel_id=1, replica_groups=mesh['row'=16,'col'=8] {'row','col'}, dimensions={0}, use_global_device_ids=true | all-gather | bytes 12384 | tf_op jit(solution)/shard_map/all_gather | solution.py:60
  317.2 44.9 %all_to_all.23 = bf16[64,128,128]{2,0,1:T(8,128)(2,1)S(1)} all-to-all(bf16[64,128,128]{2,0,1:T(8,128)(2,1)S(1)} %copy.130), channel_id=1, replica_groups=mesh['row'=16,'col'=8] {'row'}, dimensions={1} | all-to-all | bytes 4194304 | tf_op jit(solution)/shard_map/all_to_all | solution.py:85
  364.9 6.8 multiply_reduce_fusion.1
  376.9 3.3 fusion.28
  380.3 9.3 convolution_bitcast_fusion
  391.3 63.1 %all-reduce = s32[1024]{0:T(1024)S(1)} all-reduce(s32[1024]{0:T(1024)S(1)} %dynamic-update-slice), channel_id=1, replica_groups=mesh['row'=16,'col'=8] {'row','col'}, use_global_device_ids=true, to_apply=%add | all-reduce | flops 1024 | bytes 8192
  454.9 6.1 fusion.30
  461.0 8.0 fusion.48
  472.9 11.7 %reshape.172 = bf16[1024,8,4,32]{3,2,1,0:T(4,128)(2,1)} reshape(bf16[8192,128]{1,0:T(8,128)(2,1)} %get-tuple-element.162) | data formatting | bytes 4194304 | tf_op jit(solution)/shard_map/reshape | solution.py:95
  484.6 12.2 %copy.146 = bf16[8,1024,4,32]{1,3,2,0:T(8,128)(2,1)} copy(bf16[8,1024,4,32]{3,2,0,1:T(4,128)(2,1)} %bitcast.133) | data formatting | bytes 4194304 | tf_op jit(solution)/shard_map/while | solution.py:116
  496.8 6.1 reshape.173
  502.9 12.2 %copy.147 = bf16[8,1024,4,32]{1,3,2,0:T(8,128)(2,1)} copy(bf16[8,1024,4,32]{3,2,0,1:T(4,128)(2,1)} %bitcast.134) | data formatting | bytes 4194304 | tf_op jit(solution)/shard_map/while | solution.py:116
  517.7 6.1 reshape.171
  523.8 12.3 %copy.145 = bf16[8,1024,4,32]{1,3,2,0:T(8,128)(2,1)} copy(bf16[8,1024,4,32]{3,2,0,1:T(4,128)(2,1)} %bitcast.135) | data formatting | bytes 4194304 | tf_op jit(solution)/shard_map/while | solution.py:116
  536.0 172.7 %all-gather.3.cloned.1.call-done = f32[4,1024,1024]{1,0,2:T(4,128)} async-done(((f32[4,1024,8]{1,0,2:T(4,128)}), f32[4,1024,1024]{1,0,2:T(4,128)}) %all-gather.3.cloned.1.call-update) | async-done | bytes 16777232 | tf_op jit(solution)/shard_map/all_gather | solution.py:104
  708.7 17.7 %copy.144 = f32[4,1024,8,16,8]{1,4,3,2,0:T(8,128)} copy(f32[4,1024,8,16,8]{1,0,4,2,3:T(4,128)} %bitcast.138) | data formatting | bytes 33554432 | tf_op jit(solution)/shard_map/transpose | solution.py:107
  726.4 297.7 %while.21 = (s32[]{:T(128)}, f32[8,1024,4,32]{3,2,1,0:T(4,128)}, bf16[8,1024,4,32]{1,3,2,0:T(8,128)(2,1)}, bf16[8,1024,4,32]{1,3,2,0:T(8,128)(2,1)}, bf16[8,1024...) while((s32[]{:T(128)}, f32[8,1024,4,32]{3,2,1,0:T(4,128)}, ...), condition=%wide.region_9.10_spmd, body=%wide.region_4.9_spmd.sunk | while | flops 421531648 | bytes 23358848 | solution.py:116
  728.7 32.8 %while.22 = (s32[]{:T(128)}, f32[2,512,4,32]{1,3,2,0:T(8,128)S(1)}, s32[2]{0:T(128)S(1)}, bf16[1024,4,32]{0,2,1:T(8,128)(2,1)S(1)}, bf16[1024,4,32]{0,2,1:T(8,12...) while((s32[]{:T(128)}, f32[2,512,4,32]{1,3,2,0:T(8,128)S(1)}, ...), condition=%wide.region_8.8_spmd, body=%wide.region_5.7_spmd.sunk | while | flops 421531648 | bytes 18115228 | solution.py:40
  731.3 5.7 fusion.70
  736.9 8.2 fusion.71
  747.7 5.6 fusion.70
  753.3 8.1 fusion.71
  765.9 32.8 %while.22 = (s32[]{:T(128)}, f32[2,512,4,32]{1,3,2,0:T(8,128)S(1)}, s32[2]{0:T(128)S(1)}, bf16[1024,4,32]{0,2,1:T(8,128)(2,1)S(1)}, bf16[1024,4,32]{0,2,1:T(8,12...) while((s32[]{:T(128)}, f32[2,512,4,32]{1,3,2,0:T(8,128)S(1)}, ...), condition=%wide.region_8.8_spmd, body=%wide.region_5.7_spmd.sunk | while | flops 421531648 | bytes 18115228 | solution.py:40
  768.5 5.7 fusion.70
  774.1 8.2 fusion.71
  784.9 5.6 fusion.70
  790.5 8.1 fusion.71
  803.0 32.8 %while.22 = (s32[]{:T(128)}, f32[2,512,4,32]{1,3,2,0:T(8,128)S(1)}, s32[2]{0:T(128)S(1)}, bf16[1024,4,32]{0,2,1:T(8,128)(2,1)S(1)}, bf16[1024,4,32]{0,2,1:T(8,12...) while((s32[]{:T(128)}, f32[2,512,4,32]{1,3,2,0:T(8,128)S(1)}, ...), condition=%wide.region_8.8_spmd, body=%wide.region_5.7_spmd.sunk | while | flops 421531648 | bytes 18115228 | solution.py:40
  805.6 5.7 fusion.70
  811.3 8.2 fusion.71
  822.0 5.6 fusion.70
  827.7 8.1 fusion.71
  840.2 32.8 %while.22 = (s32[]{:T(128)}, f32[2,512,4,32]{1,3,2,0:T(8,128)S(1)}, s32[2]{0:T(128)S(1)}, bf16[1024,4,32]{0,2,1:T(8,128)(2,1)S(1)}, bf16[1024,4,32]{0,2,1:T(8,12...) while((s32[]{:T(128)}, f32[2,512,4,32]{1,3,2,0:T(8,128)S(1)}, ...), condition=%wide.region_8.8_spmd, body=%wide.region_5.7_spmd.sunk | while | flops 421531648 | bytes 18115228 | solution.py:40
  842.8 5.7 fusion.70
  848.5 8.2 fusion.71
  859.2 5.6 fusion.70
  864.9 8.1 fusion.71
  877.4 32.8 %while.22 = (s32[]{:T(128)}, f32[2,512,4,32]{1,3,2,0:T(8,128)S(1)}, s32[2]{0:T(128)S(1)}, bf16[1024,4,32]{0,2,1:T(8,128)(2,1)S(1)}, bf16[1024,4,32]{0,2,1:T(8,12...) while((s32[]{:T(128)}, f32[2,512,4,32]{1,3,2,0:T(8,128)S(1)}, ...), condition=%wide.region_8.8_spmd, body=%wide.region_5.7_spmd.sunk | while | flops 421531648 | bytes 18115228 | solution.py:40
  880.0 5.7 fusion.70
  885.7 8.2 fusion.71
  896.4 5.6 fusion.70
  902.1 8.1 fusion.71
  914.7 32.8 %while.22 = (s32[]{:T(128)}, f32[2,512,4,32]{1,3,2,0:T(8,128)S(1)}, s32[2]{0:T(128)S(1)}, bf16[1024,4,32]{0,2,1:T(8,128)(2,1)S(1)}, bf16[1024,4,32]{0,2,1:T(8,12...) while((s32[]{:T(128)}, f32[2,512,4,32]{1,3,2,0:T(8,128)S(1)}, ...), condition=%wide.region_8.8_spmd, body=%wide.region_5.7_spmd.sunk | while | flops 421531648 | bytes 18115228 | solution.py:40
  917.3 5.7 fusion.70
  922.9 8.2 fusion.71
  933.7 5.6 fusion.70
  939.3 8.1 fusion.71
  951.8 32.8 %while.22 = (s32[]{:T(128)}, f32[2,512,4,32]{1,3,2,0:T(8,128)S(1)}, s32[2]{0:T(128)S(1)}, bf16[1024,4,32]{0,2,1:T(8,128)(2,1)S(1)}, bf16[1024,4,32]{0,2,1:T(8,12...) while((s32[]{:T(128)}, f32[2,512,4,32]{1,3,2,0:T(8,128)S(1)}, ...), condition=%wide.region_8.8_spmd, body=%wide.region_5.7_spmd.sunk | while | flops 421531648 | bytes 18115228 | solution.py:40
  954.4 5.7 fusion.70
  960.1 8.2 fusion.71
  970.8 5.6 fusion.70
  976.4 8.1 fusion.71
  989.0 32.8 %while.22 = (s32[]{:T(128)}, f32[2,512,4,32]{1,3,2,0:T(8,128)S(1)}, s32[2]{0:T(128)S(1)}, bf16[1024,4,32]{0,2,1:T(8,128)(2,1)S(1)}, bf16[1024,4,32]{0,2,1:T(8,12...) while((s32[]{:T(128)}, f32[2,512,4,32]{1,3,2,0:T(8,128)S(1)}, ...), condition=%wide.region_8.8_spmd, body=%wide.region_5.7_spmd.sunk | while | flops 421531648 | bytes 18115228 | solution.py:40
  991.6 5.7 fusion.70
  997.3 8.2 fusion.71
  1008.0 5.7 fusion.70
  1013.7 8.1 fusion.71
  1024.2 15.3 %copy.148 = f32[1024,8,4,32]{3,2,1,0:T(4,128)} copy(f32[1024,8,4,32]{3,2,0,1:T(4,128)} %bitcast.139) | data formatting | bytes 8388608 | tf_op jit(solution)/shard_map/transpose | solution.py:120
  1039.5 13.5 %reshape.176 = f32[8192,128]{1,0:T(8,128)} reshape(f32[1024,8,4,32]{3,2,1,0:T(4,128)} %copy.148) | data formatting | bytes 8388608 | tf_op jit(solution)/shard_map/reshape | solution.py:120
  1052.9 5.6 convert_reduce_fusion
  1060.1 9.8 all-to-all-start.1
  1069.9 29.8 %all-to-all-done.1 = bf16[128,8,8,128]{3,2,1,0:T(8,128)(2,1)} async-done(((bf16[128,8,8,128]{3,2,1,0:T(8,128)(2,1)}), bf16[128,8,8,128]{3,2,1,0:T(8,128)(2,1)}, u32[]{:S(2)}, u32[]{:S(2)}) %all-to-all-start.1) | async-done | bytes 2097184 | tf_op jit(solution)/shard_map/all_to_all | solution.py:127
  1102.8 3.8 fusion.24
  1118.5 31.5 %all_to_all.24 = bf16[1024,8,128]{2,1,0:T(8,128)(2,1)S(1)} all-to-all(bf16[1024,8,128]{2,1,0:T(8,128)(2,1)} %bitcast.142), channel_id=1, replica_groups=mesh['row'=16,'col'=8] {'row'}, dimensions={0} | all-to-all | bytes 4194304 | tf_op jit(solution)/shard_map/all_to_all | solution.py:131
  (124 shorter events, 85.9 us)
Async XLA Ops:
  6.5 454.5 %copy-start = (bf16[128,512]{1,0:T(8,128)(2,1)S(1)}, bf16[128,512]{1,0:T(8,128)(2,1)}, u32[]{:S(2)}) copy-start(bf16[128,512]{1,0:T(8,128)(2,1)} %param.17) | copy-start | bytes 393220
  6.5 702.2 %all-gather.3.cloned.1.call-start = ((), (), s32[]{:S(2)}) async-start(), calls=%async_computation.3 | async-start | bytes 16908288 | tf_op jit(solution)/shard_map/all_gather | solution.py:104
  374.9 2.0 copy-start.2
  374.9 5.3 copy-start.5
  380.2 10.8 copy-start.8
  469.0 3.8 copy-start.3
  1039.5 13.5 %copy-start.6 = (bf16[128,128]{1,0:T(8,128)(2,1)S(1)}, bf16[128,128]{1,0:T(8,128)(2,1)}, u32[]{:S(2)}) copy-start(bf16[128,128]{1,0:T(8,128)(2,1)} %param.19) | copy-start | bytes 98308
  1060.1 39.7 %all-to-all-start.1 = ((bf16[128,8,8,128]{3,2,1,0:T(8,128)(2,1)}), bf16[128,8,8,128]{3,2,1,0:T(8,128)(2,1)}, u32[]{:S(2)}, u32[]{:S(2)}) async-start(bf16[128,8,8,128]{3,2,1,0:T(8,128)(2,1)} %bitcast.141), calls=%async_computation.1 | async-start | bytes 4194304 | tf_op jit(solution)/shard_map/all_to_all | solution.py:127
  1106.6 3.0 copy-start.7
  1106.6 6.1 copy-start.4
  1118.5 34.0 %copy-start.1 = (bf16[128,512]{1,0:T(8,128)(2,1)S(1)}, bf16[128,512]{1,0:T(8,128)(2,1)}, u32[]{:S(2)}) copy-start(bf16[128,512]{1,0:T(8,128)(2,1)} %param.17) | copy-start | bytes 393220
Sparse Core Ops, SparseCore 0:
  391.1 317.5 all-gather.2
where the time goes:
time: 1170 us; the launch traced here: 1160 us
  blocking collectives  445 us (38%)
  matrix products  253 us (22%)
  waiting for transfers between devices  203 us (17%)
  local copies, waits for them, and re-layouts  170 us (15%)
  other arithmetic  33.9 us (3%)
  loops' own time  31.2 us (3%)
  between operations  14 us (1%)
    all_gather x1, blocking collectives, per_device(): lax.all_gather(coords, ('row', 'col'), axis=1, tiled=True)  306 us
    all_gather x1, waiting for transfers between devices, per_device(): gathered = lax.all_gather(bias_local, ('row', 'col'), axis=2, tiled=True)  173 us
    dot_general x16, matrix products, one_block(): jnp.einsum('hki,khd->ihd', weights, value_rows, preferred_element_type=jn...  130 us
    sub x16, matrix products, one_block(): raised = jnp.exp(scores - highest)  90.4 us
    unnamed x1, blocking collectives  63.1 us
    all_to_all x1, blocking collectives, per_device(): lax.all_to_all(pair, 'row', split_axis=1, concat_axis=0, tiled=True)  44.9 us
    while x3, local copies, waits for them, and re-layouts, per_device(): lax.map(one_column, (jnp.swapaxes(query_all, 0, 1), jnp.swapaxes(key_all,...  36.7 us
    all_to_all x1, blocking collectives, per_device(): lax.all_to_all(logits_cols.astype(jnp.bfloat16), 'row', split_axis=0, con...  31.5 us
  transfers between devices with their start and end apart: 2, of which 2 were waited for; matrix products, arithmetic and copies ran while one was open for 7% of the time, Pallas kernels for 0%

commit v1 on v0

--- a/solution.py
+++ b/solution.py
@@ -101,7 +101,12 @@
     )
     gate_all = projected[:, 3 * width :].astype(jnp.bfloat16)
     bias_local = jnp.einsum("kic,ch->hki", normed, w_bias, preferred_element_type=jnp.float32)
-    gathered = lax.all_gather(bias_local, ("row", "col"), axis=2, tiled=True)
+    gathered = jnp.concatenate(
+        lax.all_to_all(
+            jnp.stack([bias_local] * lax.axis_size(("row", "col"))), ("row", "col"), 0, 0
+        ),
+        axis=2,
+    )
     bias_full = (
         gathered.reshape(heads, total, n_rows, n_cols, slab)
         .transpose(0, 1, 3, 2, 4)

time: 1170 us -> 1210 us (1.034)
  blocking collectives: 445 us -> 674 us
  waiting for transfers between devices: 203 us -> 29.8 us
  between operations: 14 us -> 0.59 us
    unnamed x1, blocking collectives: 63.1 us -> 292 us
    all_gather x1 -> x0, waiting for transfers between devices: 173 us -> none  [per_device(): gathered = lax.all_gather(bias_local, ('row', 'col'), axis=2, tiled=True)]
  transfers between devices with their start and end apart: 2 -> 2, of which waited for: 2 -> 1; matrix products, arithmetic and copies ran while one was open for 7% -> 7% of each run, Pallas kernels for 0% -> 0%
where the time goes in v1:
time: 1210 us
  blocking collectives  674 us (56%)
  matrix products  253 us (21%)
  local copies, waits for them, and re-layouts  171 us (14%)
  other arithmetic  33.9 us (3%)
  loops' own time  31.2 us (3%)
  waiting for transfers between devices  29.8 us (2%)
  starting transfers between devices  12.3 us (1%)
    all_gather x1, blocking collectives, per_device(): lax.all_gather(coords, ('row', 'col'), axis=1, tiled=True)  306 us
    unnamed x1, blocking collectives  292 us
    dot_general x16, matrix products, one_block(): jnp.einsum('hki,khd->ihd', weights, value_rows, preferred_element_type=jn...  130 us
    sub x16, matrix products, one_block(): raised = jnp.exp(scores - highest)  90.6 us
    all_to_all x1, blocking collectives, per_device(): lax.all_to_all(pair, 'row', split_axis=1, concat_axis=0, tiled=True)  44.9 us
    while x3, local copies, waits for them, and re-layouts, per_device(): lax.map(one_column, (jnp.swapaxes(query_all, 0, 1), jnp.swapaxes(key_all,...  36.7 us
    all_to_all x1, blocking collectives, per_device(): lax.all_to_all(logits_cols.astype(jnp.bfloat16), 'row', split_axis=0, con...  31.5 us
    another operation x8, loops' own time, attend_column(): blocks_out = lax.map(one_block, starts)  30.7 us
  transfers between devices with their start and end apart: 2, of which 1 were waited for; matrix products, arithmetic and copies ran while one was open for 7% of the time, Pallas kernels for 0%

profile of v1, /device:TPU:1, one launch (start us, length us, event | category | flops | bytes accessed | tf_op | source)
XLA Modules:
  0.0 1205.4 jit_solution(2378054919660747114)
XLA Ops:
  0.0 305.9 %all-gather = s32[128,8,3]{1,2,0:T(4,128)S(1)} all-gather(s32[1,8,3]{1,2,0:T(4,128)} %bitcast.145), channel_id=1, replica_groups=mesh['row'=16,'col'=8] {'row','col'}, dimensions={0}, use_global_device_ids=true | all-gather | bytes 12384 | tf_op jit(solution)/shard_map/all_gather | solution.py:60
  310.7 44.9 %all_to_all.28 = bf16[64,128,128]{2,0,1:T(8,128)(2,1)S(1)} all-to-all(bf16[64,128,128]{2,0,1:T(8,128)(2,1)S(1)} %copy.154), channel_id=1, replica_groups=mesh['row'=16,'col'=8] {'row'}, dimensions={1} | all-to-all | bytes 4194304 | tf_op jit(solution)/shard_map/all_to_all | solution.py:85
  358.4 6.8 multiply_reduce_fusion.1
  373.7 9.3 convolution_bitcast_fusion
  383.9 7.9 stack.2
  391.8 6.1 all-to-all-start.1
  398.2 291.5 %all-reduce = s32[1024]{0:T(1024)S(1)} all-reduce(s32[1024]{0:T(1024)S(1)} %dynamic-update-slice), channel_id=1, replica_groups=mesh['row'=16,'col'=8] {'row','col'}, use_global_device_ids=true, to_apply=%add | all-reduce | flops 1024 | bytes 8192
  690.3 6.1 fusion.30
  696.4 8.0 fusion.48
  708.2 11.7 reshape.174
  719.9 12.2 %copy.171 = bf16[8,1024,4,32]{1,3,2,0:T(8,128)(2,1)} copy(bf16[8,1024,4,32]{3,2,0,1:T(4,128)(2,1)} %bitcast.134) | data formatting | bytes 4194304 | tf_op jit(solution)/shard_map/while | solution.py:121
  732.2 6.1 reshape.175
  738.3 12.2 %copy.172 = bf16[8,1024,4,32]{1,3,2,0:T(8,128)(2,1)} copy(bf16[8,1024,4,32]{3,2,0,1:T(4,128)(2,1)} %bitcast.135) | data formatting | bytes 4194304 | tf_op jit(solution)/shard_map/while | solution.py:121
  753.0 6.0 reshape.173
  759.0 12.2 %copy.170 = bf16[8,1024,4,32]{1,3,2,0:T(8,128)(2,1)} copy(bf16[8,1024,4,32]{3,2,0,1:T(4,128)(2,1)} %bitcast.136) | data formatting | bytes 4194304 | tf_op jit(solution)/shard_map/while | solution.py:121
  771.3 11.8 copy.169
  783.1 297.3 %while.21 = (s32[]{:T(128)}, f32[8,1024,4,32]{3,2,1,0:T(4,128)}, bf16[8,1024,4,32]{1,3,2,0:T(8,128)(2,1)}, bf16[8,1024,4,32]{1,3,2,0:T(8,128)(2,1)}, bf16[8,1024...) while((s32[]{:T(128)}, f32[8,1024,4,32]{3,2,1,0:T(4,128)}, ...), condition=%wide.region_9.10_spmd, body=%wide.region_4.9_spmd.sunk | while | flops 421531648 | bytes 23358848 | solution.py:121
  785.3 32.7 %while.22 = (s32[]{:T(128)}, f32[2,512,4,32]{1,3,2,0:T(8,128)S(1)}, s32[2]{0:T(128)S(1)}, bf16[1024,4,32]{0,2,1:T(8,128)(2,1)S(1)}, bf16[1024,4,32]{0,2,1:T(8,12...) while((s32[]{:T(128)}, f32[2,512,4,32]{1,3,2,0:T(8,128)S(1)}, ...), condition=%wide.region_8.8_spmd, body=%wide.region_5.7_spmd.sunk | while | flops 421531648 | bytes 18115228 | solution.py:40
  787.9 5.7 fusion.70
  793.6 8.2 fusion.71
  804.3 5.7 fusion.70
  809.9 8.1 fusion.71
  822.5 32.7 %while.22 = (s32[]{:T(128)}, f32[2,512,4,32]{1,3,2,0:T(8,128)S(1)}, s32[2]{0:T(128)S(1)}, bf16[1024,4,32]{0,2,1:T(8,128)(2,1)S(1)}, bf16[1024,4,32]{0,2,1:T(8,12...) while((s32[]{:T(128)}, f32[2,512,4,32]{1,3,2,0:T(8,128)S(1)}, ...), condition=%wide.region_8.8_spmd, body=%wide.region_5.7_spmd.sunk | while | flops 421531648 | bytes 18115228 | solution.py:40
  825.0 5.7 fusion.70
  830.7 8.2 fusion.71
  841.4 5.7 fusion.70
  847.1 8.1 fusion.71
  859.6 32.7 %while.22 = (s32[]{:T(128)}, f32[2,512,4,32]{1,3,2,0:T(8,128)S(1)}, s32[2]{0:T(128)S(1)}, bf16[1024,4,32]{0,2,1:T(8,128)(2,1)S(1)}, bf16[1024,4,32]{0,2,1:T(8,12...) while((s32[]{:T(128)}, f32[2,512,4,32]{1,3,2,0:T(8,128)S(1)}, ...), condition=%wide.region_8.8_spmd, body=%wide.region_5.7_spmd.sunk | while | flops 421531648 | bytes 18115228 | solution.py:40
  862.1 5.7 fusion.70
  867.8 8.2 fusion.71
  878.5 5.6 fusion.70
  884.1 8.1 fusion.71
  896.7 32.7 %while.22 = (s32[]{:T(128)}, f32[2,512,4,32]{1,3,2,0:T(8,128)S(1)}, s32[2]{0:T(128)S(1)}, bf16[1024,4,32]{0,2,1:T(8,128)(2,1)S(1)}, bf16[1024,4,32]{0,2,1:T(8,12...) while((s32[]{:T(128)}, f32[2,512,4,32]{1,3,2,0:T(8,128)S(1)}, ...), condition=%wide.region_8.8_spmd, body=%wide.region_5.7_spmd.sunk | while | flops 421531648 | bytes 18115228 | solution.py:40
  899.2 5.7 fusion.70
  904.9 8.2 fusion.71
  915.6 5.7 fusion.70
  921.3 8.1 fusion.71
  933.8 32.7 %while.22 = (s32[]{:T(128)}, f32[2,512,4,32]{1,3,2,0:T(8,128)S(1)}, s32[2]{0:T(128)S(1)}, bf16[1024,4,32]{0,2,1:T(8,128)(2,1)S(1)}, bf16[1024,4,32]{0,2,1:T(8,12...) while((s32[]{:T(128)}, f32[2,512,4,32]{1,3,2,0:T(8,128)S(1)}, ...), condition=%wide.region_8.8_spmd, body=%wide.region_5.7_spmd.sunk | while | flops 421531648 | bytes 18115228 | solution.py:40
  936.4 5.7 fusion.70
  942.1 8.2 fusion.71
  952.8 5.7 fusion.70
  958.4 8.1 fusion.71
  971.0 32.7 %while.22 = (s32[]{:T(128)}, f32[2,512,4,32]{1,3,2,0:T(8,128)S(1)}, s32[2]{0:T(128)S(1)}, bf16[1024,4,32]{0,2,1:T(8,128)(2,1)S(1)}, bf16[1024,4,32]{0,2,1:T(8,12...) while((s32[]{:T(128)}, f32[2,512,4,32]{1,3,2,0:T(8,128)S(1)}, ...), condition=%wide.region_8.8_spmd, body=%wide.region_5.7_spmd.sunk | while | flops 421531648 | bytes 18115228 | solution.py:40
  973.6 5.7 fusion.70
  979.3 8.2 fusion.71
  990.0 5.7 fusion.70
  995.6 8.1 fusion.71
  1008.2 32.7 %while.22 = (s32[]{:T(128)}, f32[2,512,4,32]{1,3,2,0:T(8,128)S(1)}, s32[2]{0:T(128)S(1)}, bf16[1024,4,32]{0,2,1:T(8,128)(2,1)S(1)}, bf16[1024,4,32]{0,2,1:T(8,12...) while((s32[]{:T(128)}, f32[2,512,4,32]{1,3,2,0:T(8,128)S(1)}, ...), condition=%wide.region_8.8_spmd, body=%wide.region_5.7_spmd.sunk | while | flops 421531648 | bytes 18115228 | solution.py:40
  1010.7 5.7 fusion.70
  1016.4 8.2 fusion.71
  1027.1 5.7 fusion.70
  1032.7 8.1 fusion.71
  1045.3 32.7 %while.22 = (s32[]{:T(128)}, f32[2,512,4,32]{1,3,2,0:T(8,128)S(1)}, s32[2]{0:T(128)S(1)}, bf16[1024,4,32]{0,2,1:T(8,128)(2,1)S(1)}, bf16[1024,4,32]{0,2,1:T(8,12...) while((s32[]{:T(128)}, f32[2,512,4,32]{1,3,2,0:T(8,128)S(1)}, ...), condition=%wide.region_8.8_spmd, body=%wide.region_5.7_spmd.sunk | while | flops 421531648 | bytes 18115228 | solution.py:40
  1047.8 5.7 fusion.70
  1053.5 8.2 fusion.71
  1064.2 5.6 fusion.70
  1069.9 8.1 fusion.71
  1080.3 15.3 %copy.173 = f32[1024,8,4,32]{3,2,1,0:T(4,128)} copy(f32[1024,8,4,32]{3,2,0,1:T(4,128)} %bitcast.139) | data formatting | bytes 8388608 | tf_op jit(solution)/shard_map/transpose | solution.py:125
  1095.6 13.5 %reshape.178 = f32[8192,128]{1,0:T(8,128)} reshape(f32[1024,8,4,32]{3,2,1,0:T(4,128)} %copy.173) | data formatting | bytes 8388608 | tf_op jit(solution)/shard_map/reshape | solution.py:125
  1109.1 5.6 convert_reduce_fusion
  1116.3 6.2 all-to-all-start.2
  1122.5 29.8 %all-to-all-done.2 = bf16[128,8,8,128]{3,2,1,0:T(8,128)(2,1)} async-done(((bf16[128,8,8,128]{3,2,1,0:T(8,128)(2,1)}), bf16[128,8,8,128]{3,2,1,0:T(8,128)(2,1)}, u32[]{:S(2)}, u32[]{:S(2)}) %all-to-all-start.2) | async-done | bytes 2097184 | tf_op jit(solution)/shard_map/all_to_all | solution.py:132
  1155.4 3.8 fusion.24
  1171.0 31.5 %all_to_all.29 = bf16[1024,8,128]{2,1,0:T(8,128)(2,1)S(1)} all-to-all(bf16[1024,8,128]{2,1,0:T(8,128)(2,1)} %bitcast.142), channel_id=1, replica_groups=mesh['row'=16,'col'=8] {'row'}, dimensions={0} | all-to-all | bytes 4194304 | tf_op jit(solution)/shard_map/all_to_all | solution.py:136
  (124 shorter events, 88.1 us)
Async XLA Ops:
  0.0 696.4 %copy-start = (bf16[128,512]{1,0:T(8,128)(2,1)S(1)}, bf16[128,512]{1,0:T(8,128)(2,1)}, u32[]{:S(2)}) copy-start(bf16[128,512]{1,0:T(8,128)(2,1)} %param.17) | copy-start | bytes 393220
  368.4 2.0 copy-start.2
  368.4 5.3 copy-start.5
  391.8 6.2 copy-start.8
  391.8 379.5 %all-to-all-start.1 = ((f32[128,4,1024,8]{2,3,1,0:T(8,128)}), f32[128,4,1024,8]{2,3,1,0:T(8,128)}, u32[]{:S(2)}, u32[]{:S(2)}) async-start(f32[128,4,1024,8]{2,3,1,0:T(8,128)} %stack.2), calls=%async_computation.1 | async-start | bytes 33554432 | tf_op jit(solution)/shard_map/all_to_all | solution.py:105
  704.4 3.8 copy-start.3
  1095.6 13.5 %copy-start.6 = (bf16[128,128]{1,0:T(8,128)(2,1)S(1)}, bf16[128,128]{1,0:T(8,128)(2,1)}, u32[]{:S(2)}) copy-start(bf16[128,128]{1,0:T(8,128)(2,1)} %param.19) | copy-start | bytes 98308
  1116.3 36.0 %all-to-all-start.2 = ((bf16[128,8,8,128]{3,2,1,0:T(8,128)(2,1)}), bf16[128,8,8,128]{3,2,1,0:T(8,128)(2,1)}, u32[]{:S(2)}, u32[]{:S(2)}) async-start(bf16[128,8,8,128]{3,2,1,0:T(8,128)(2,1)} %bitcast.141), calls=%async_computation.2 | async-start | bytes 4194304 | tf_op jit(solution)/shard_map/all_to_all | solution.py:132
  1159.2 3.0 copy-start.7
  1159.2 6.1 copy-start.4
  1171.0 34.0 %copy-start.1 = (bf16[128,512]{1,0:T(8,128)(2,1)S(1)}, bf16[128,512]{1,0:T(8,128)(2,1)}, u32[]{:S(2)}) copy-start(bf16[128,512]{1,0:T(8,128)(2,1)} %param.17) | copy-start | bytes 393220
